TPU v7x, 128 devices: a whole 4x4x4 slice. The times are simulated.
128 devices in a mesh: img: 2 (over core), band: 64 (over z, y, x).
Axes of the slice: x: 4, y: 4, z: 4, core: 2. Of those that a mesh axis runs over, the one named last changes fastest.
Arguments:
- latent: bfloat16 [8, 256, 32, 1280], P('img', 'band'), parts along dimension 0, may hold values from -80 to 80
- stale_act: bfloat16 [8, 256, 32, 1280], P('img', 'band'), parts along dimension 0, may hold values from -4 to 4
- stale_kv: bfloat16 [2, 8, 256, 32, 640], P(None, 'img', 'band'), parts along dimension 1, may hold values from -600 to 600
- timestep: int32 [8, 8], P('img'), parts along dimension 0, may hold values from 0 to 999
- norm_gain: float32 [1280], replicated, may hold values from 0.1 to 1.9
- norm_shift: float32 [1280], replicated, may hold values from -1 to 1
- conv_weight: bfloat16 [3, 3, 1280, 640], replicated, may hold values from -0.0546875 to 0.0546875
- time_weight: bfloat16 [1280, 640], replicated, may hold values from -0.15625 to 0.15625
- attn_in: bfloat16 [1280, 1920], replicated, may hold values from -0.15625 to 0.15625
- attn_out: bfloat16 [640, 1280], replicated, may hold values from -0.25 to 0.25
Outputs:
- block_out: bfloat16 [8, 256, 32, 1280], P('img', 'band'), parts along dimension 0
- fresh_kv: bfloat16 [2, 8, 256, 32, 640], P(None, 'img', 'band'), parts along dimension 1
There are 2 independent parts, one for each index of `img`. A program takes and returns all parts, laid end to end along the dimension named above; an argument that names none is the same for every part. Nothing has to cross between parts.
All inputs are finite; a program needn't handle non-finite values.
Results may differ from a plain program's by a relative error of at most 0.0055.
Values may be sent and summed in bfloat16 or wider, within the bound.
No kernel may reach another device: no remote copies, remote signals or barrier semaphores. Data moves between devices by JAX's collectives and lax.ppermute only.
A program may use at most 192 MiB of HBM per device.

v0:
```python
import math
import jax
import jax.numpy as jnp
from jax import lax
from jax.sharding import PartitionSpec as P

IMG_ROWS = 32
GROUPS = 32
HEADS = 10
TDIM = 1280


def shifted(value, axis, by):
    count = lax.axis_size(axis)
    pairs = [(i, i + by) for i in range(count) if 0 <= i + by < count]
    return lax.ppermute(value, axis, pairs)


def time_term(timestep, time_weight):
    half_dim = TDIM // 2
    frequency = jnp.exp(-math.log(10000.0) * jnp.arange(half_dim, dtype=jnp.float32) / half_dim)
    angles = timestep.astype(jnp.float32)[:, None] * frequency[None, :]
    embedding = jnp.concatenate([jnp.cos(angles), jnp.sin(angles)], axis=1)
    return jnp.dot(
        jax.nn.silu(embedding), time_weight.astype(jnp.float32), precision=lax.Precision.HIGHEST
    )


def attend_block(queries, keys, values, scale_factor):
    scores = (
        jnp.einsum("bqhd,bkhd->bhqk", queries, keys, preferred_element_type=jnp.float32)
        * scale_factor
    )
    peak = jnp.max(scores, axis=-1)
    exponent = jnp.exp(scores - peak[..., None])
    context = jnp.einsum(
        "bhqk,bkhd->bhqd", exponent.astype(jnp.bfloat16), values, preferred_element_type=jnp.float32
    )
    return (peak, jnp.sum(exponent, axis=-1), context)


def on_device(
    latent,
    stale_act,
    stale_kv,
    timestep,
    norm_gain,
    norm_shift,
    conv_weight,
    time_weight,
    attn_in,
    attn_out,
):
    images, height, columns, channels = latent.shape
    conv_width = conv_weight.shape[3]
    inner_width = attn_out.shape[0]
    head_count = HEADS
    head_size = inner_width // head_count
    per_group = channels // GROUPS
    group_size = IMG_ROWS // height
    band_count = lax.axis_size("band")
    stacked = band_count * height // IMG_ROWS
    band_index = lax.axis_index("band")
    slot = band_index % stacked
    place = band_index // stacked
    slot_mask = (jnp.arange(stacked) == slot).astype(jnp.float32)[:, None, None]
    counted = float(IMG_ROWS * columns * per_group)
    floats = latent.astype(jnp.float32)
    grouped = floats.reshape(images, height * columns, GROUPS, per_group)
    totals = lax.psum(slot_mask * jnp.sum(grouped, axis=(1, 3))[None], "band")
    center = jnp.sum(totals * slot_mask, axis=0) / counted
    deviation = grouped - center[:, None, :, None]
    spreads = lax.psum(slot_mask * jnp.sum(deviation * deviation, axis=(1, 3))[None], "band")
    spread = jnp.sum(spreads * slot_mask, axis=0) / counted
    normed = (
        (grouped - center[:, None, :, None]) / jnp.sqrt(spread + 1e-05)[:, None, :, None]
    ).reshape(latent.shape)
    activated = jax.nn.silu(normed * norm_gain + norm_shift).astype(jnp.bfloat16)
    top_rim = shifted(stale_act[:, height - 1 :], "band", stacked)
    bottom_rim = shifted(stale_act[:, :1], "band", -stacked)
    top_rim = jnp.where(place == 0, jnp.zeros_like(top_rim), top_rim)
    bottom_rim = jnp.where(place == group_size - 1, jnp.zeros_like(bottom_rim), bottom_rim)
    extended = jnp.concatenate([top_rim, activated, bottom_rim], axis=1)
    padded = jnp.pad(extended, ((0, 0), (0, 0), (1, 1), (0, 0)))
    convolved = jnp.zeros((images, height, columns, conv_width), jnp.float32)
    for row_tap in range(3):
        for col_tap in range(3):
            convolved = convolved + jnp.einsum(
                "bhwc,cd->bhwd",
                padded[:, row_tap : row_tap + height, col_tap : col_tap + columns],
                conv_weight[row_tap, col_tap],
                preferred_element_type=jnp.float32,
            )
    own_steps = lax.dynamic_index_in_dim(timestep, slot, 1, keepdims=False)
    time_bias = time_term(own_steps, time_weight)
    window = (floats[..., :conv_width] + convolved + time_bias[:, None, None, :]).astype(
        jnp.bfloat16
    )
    hidden = jnp.concatenate([window, latent[..., conv_width:]], axis=-1)
    widened = hidden.astype(jnp.float32)
    token_mean = jnp.mean(widened, axis=-1, keepdims=True)
    token_var = jnp.mean((widened - token_mean) ** 2, axis=-1, keepdims=True)
    normalized = ((widened - token_mean) / jnp.sqrt(token_var + 1e-05)).astype(jnp.bfloat16)
    projected = jnp.dot(
        normalized.reshape(-1, channels), attn_in, preferred_element_type=jnp.float32
    )
    projected = projected.astype(jnp.bfloat16).reshape(images, height, columns, 3 * inner_width)
    fresh_kv = jnp.stack(
        [projected[..., inner_width : 2 * inner_width], projected[..., 2 * inner_width :]]
    )
    tokens_dev = height * columns
    query_heads = projected[..., :inner_width].reshape(images, tokens_dev, head_count, head_size)
    fresh_keys = fresh_kv[0].reshape(images, tokens_dev, head_count, head_size)
    fresh_values = fresh_kv[1].reshape(images, tokens_dev, head_count, head_size)
    scale_factor = head_size ** (-0.5)
    start_carry = attend_block(query_heads, fresh_keys, fresh_values, scale_factor)

    def absorb(carry, piece):
        running_max, running_sum, context = carry
        piece_rows = piece.shape[2]
        piece_keys = piece[0].reshape(images, piece_rows * columns, head_count, head_size)
        piece_values = piece[1].reshape(images, piece_rows * columns, head_count, head_size)
        peak, total, partial_ctx = attend_block(query_heads, piece_keys, piece_values, scale_factor)
        new_max = jnp.maximum(running_max, peak)
        old_factor = jnp.exp(running_max - new_max)
        new_factor = jnp.exp(peak - new_max)
        return (
            new_max,
            running_sum * old_factor + total * new_factor,
            context * old_factor[..., None] + partial_ctx * new_factor[..., None],
        )

    def chain_step(step, state):
        upward, downward, carry = state
        upward = shifted(upward, "band", stacked)
        downward = shifted(downward, "band", -stacked)
        carry = lax.cond(place >= step, lambda held: absorb(held, upward), lambda held: held, carry)
        carry = lax.cond(
            place + step < group_size, lambda held: absorb(held, downward), lambda held: held, carry
        )
        return (upward, downward, carry)

    final_state = lax.fori_loop(1, group_size, chain_step, (stale_kv, stale_kv, start_carry))
    running_max, running_sum, context = final_state[2]
    attended = jnp.transpose(context / running_sum[..., None], (0, 2, 1, 3)).astype(jnp.bfloat16)
    update = jnp.dot(
        attended.reshape(-1, inner_width), attn_out, preferred_element_type=jnp.float32
    )
    block_out = (widened + update.reshape(images, height, columns, channels)).astype(jnp.bfloat16)
    return (block_out, fresh_kv)


def solution(mesh):
    return jax.shard_map(
        on_device,
        mesh=mesh,
        in_specs=(
            P("img", "band", None, None),
            P("img", "band", None, None),
            P(None, "img", "band", None, None),
            P("img", None),
            P(),
            P(),
            P(),
            P(),
            P(),
            P(),
        ),
        out_specs=(P("img", "band", None, None), P(None, "img", "band", None, None)),
        check_vma=False,
    )
```

profile of v0, /device:TPU:0, one launch (start us, length us, event | category | flops | bytes accessed | tf_op | source)
XLA Modules:
  0.0 1268.4 jit_solution(8291177125210356071)
XLA Ops:
  14.5 351.0 %psum.14 = f32[8,4,32]{2,0,1:T(8,128)S(1)} all-reduce(f32[8,4,32]{2,0,1:T(8,128)S(1)} %broadcast_multiply_fusion.1), channel_id=1, replica_groups=mesh['img'=2,'band'=64] {'band'}, use_global_device_ids=true, to_apply=%region_2.3 | all-reduce | flops 1024 | bytes 8192 | tf_op jit(solution)/shard_map/psum | solution.py:70
  366.5 341.7 %psum.15 = f32[8,4,32]{2,0,1:T(8,128)S(1)} all-reduce(f32[8,4,32]{2,0,1:T(8,128)S(1)} %broadcast_multiply_fusion), channel_id=1, replica_groups=mesh['img'=2,'band'=64] {'band'}, use_global_device_ids=true, to_apply=%region_6.7 | all-reduce | flops 1024 | bytes 8192 | tf_op jit(solution)/shard_map/psum | solution.py:73
  753.3 502.6 %while.21 = (s32[]{:T(128)}, bf16[2,4,4,32,640]{4,3,2,1,0:T(8,128)(2,1)}, bf16[2,4,4,32,640]{4,3,2,1,0:T(8,128)(2,1)}, f32[4,10,128]{2,1,0:T(8,128)S(1)}, f32[4,...) while((s32[]{:T(128)}, ...), condition=%wide.region_21.22_spmd, body=%wide.region_12.21_spmd.sunk | while | flops 348037120 | bytes 72663480 | solution.py:143
  757.0 26.2 %collective-permute-done = bf16[2,4,4,32,640]{4,3,2,1,0:T(8,128)(2,1)} collective-permute-done((bf16[2,4,4,32,640]{4,3,2,1,0:T(8,128)(2,1)}, bf16[2,4,4,32,640]{4,3,2,1,0:T(8,128)(2,1)}, u32[]{:S(2)}, u32[]{:S(2)}) %collective-permute-start) | collective-permute-done | bytes 1310752 | tf_op jit(solution)/shard_map/while/body/eval_jaxpr/ppermute | solution.py:16
  789.0 17.1 %conditional.5 = ((f32[4,10,128]{2,1,0:T(8,128)S(1)}, f32[4,10,128]{2,1,0:T(8,128)S(1)}, f32[4,10,128,64]{2,3,1,0:T(8,128)S(1)})) conditional(s32[]{:T(128)} %convert_element_type.114, (f32[4,10,128]{2,1,0:T(8,128)S(1)}, f32[4,10,128]{2,1,0:T(8,128)S(1)}, f32[4,10,128,64]{2,3,1,0:T(8,128)S(1)}) %get-tuple-element.368, ...), branch_computations={%region_17.17_spmd, %region_18.20_spmd} | conditional | flops 174018560 | bytes 28467260 | solution.py:138
  811.1 18.4 %collective-permute-start = (bf16[2,4,4,32,640]{4,3,2,1,0:T(8,128)(2,1)}, bf16[2,4,4,32,640]{4,3,2,1,0:T(8,128)(2,1)}, u32[]{:S(2)}, u32[]{:S(2)}) collective-permute-start(bf16[2,4,4,32,640]{4,3,2,1,0:T(8,128)(2,1)} %get-tuple-element.349), channel_id=1, source_target_pairs={{0,8},{1,9},{2,10},{3,11},{4,12},{5,13},{6,14},{7,15},{8,16},{9,17... | collective-permute-start | bytes 3932168 | tf_op jit(solution)/shard_map/while/body/eval_jaxpr/ppermute | solution.py:16
  830.8 26.5 %collective-permute-done = bf16[2,4,4,32,640]{4,3,2,1,0:T(8,128)(2,1)} collective-permute-done((bf16[2,4,4,32,640]{4,3,2,1,0:T(8,128)(2,1)}, bf16[2,4,4,32,640]{4,3,2,1,0:T(8,128)(2,1)}, u32[]{:S(2)}, u32[]{:S(2)}) %collective-permute-start) | collective-permute-done | bytes 1310752 | tf_op jit(solution)/shard_map/while/body/eval_jaxpr/ppermute | solution.py:16
  857.3 28.8 %collective-permute-done.1 = bf16[2,4,4,32,640]{4,3,2,1,0:T(8,128)(2,1)} collective-permute-done((bf16[2,4,4,32,640]{4,3,2,1,0:T(8,128)(2,1)}, bf16[2,4,4,32,640]{4,3,2,1,0:T(8,128)(2,1)}, u32[]{:S(2)}, u32[]{:S(2)}) %collective-permute-start.1) | collective-permute-done | bytes 1310752 | tf_op jit(solution)/shard_map/while/body/eval_jaxpr/ppermute | solution.py:16
  886.2 17.1 %conditional.5 = ((f32[4,10,128]{2,1,0:T(8,128)S(1)}, f32[4,10,128]{2,1,0:T(8,128)S(1)}, f32[4,10,128,64]{2,3,1,0:T(8,128)S(1)})) conditional(s32[]{:T(128)} %convert_element_type.114, (f32[4,10,128]{2,1,0:T(8,128)S(1)}, f32[4,10,128]{2,1,0:T(8,128)S(1)}, f32[4,10,128,64]{2,3,1,0:T(8,128)S(1)}) %get-tuple-element.368, ...), branch_computations={%region_17.17_spmd, %region_18.20_spmd} | conditional | flops 174018560 | bytes 28467260 | solution.py:138
  912.1 26.1 %collective-permute-done = bf16[2,4,4,32,640]{4,3,2,1,0:T(8,128)(2,1)} collective-permute-done((bf16[2,4,4,32,640]{4,3,2,1,0:T(8,128)(2,1)}, bf16[2,4,4,32,640]{4,3,2,1,0:T(8,128)(2,1)}, u32[]{:S(2)}, u32[]{:S(2)}) %collective-permute-start) | collective-permute-done | bytes 1310752 | tf_op jit(solution)/shard_map/while/body/eval_jaxpr/ppermute | solution.py:16
  938.2 28.7 %collective-permute-done.1 = bf16[2,4,4,32,640]{4,3,2,1,0:T(8,128)(2,1)} collective-permute-done((bf16[2,4,4,32,640]{4,3,2,1,0:T(8,128)(2,1)}, bf16[2,4,4,32,640]{4,3,2,1,0:T(8,128)(2,1)}, u32[]{:S(2)}, u32[]{:S(2)}) %collective-permute-start.1) | collective-permute-done | bytes 1310752 | tf_op jit(solution)/shard_map/while/body/eval_jaxpr/ppermute | solution.py:16
  966.9 17.1 %conditional.5 = ((f32[4,10,128]{2,1,0:T(8,128)S(1)}, f32[4,10,128]{2,1,0:T(8,128)S(1)}, f32[4,10,128,64]{2,3,1,0:T(8,128)S(1)})) conditional(s32[]{:T(128)} %convert_element_type.114, (f32[4,10,128]{2,1,0:T(8,128)S(1)}, f32[4,10,128]{2,1,0:T(8,128)S(1)}, f32[4,10,128,64]{2,3,1,0:T(8,128)S(1)}) %get-tuple-element.368, ...), branch_computations={%region_17.17_spmd, %region_18.20_spmd} | conditional | flops 174018560 | bytes 28467260 | solution.py:138
  992.9 25.5 %collective-permute-done = bf16[2,4,4,32,640]{4,3,2,1,0:T(8,128)(2,1)} collective-permute-done((bf16[2,4,4,32,640]{4,3,2,1,0:T(8,128)(2,1)}, bf16[2,4,4,32,640]{4,3,2,1,0:T(8,128)(2,1)}, u32[]{:S(2)}, u32[]{:S(2)}) %collective-permute-start) | collective-permute-done | bytes 1310752 | tf_op jit(solution)/shard_map/while/body/eval_jaxpr/ppermute | solution.py:16
  1018.4 28.7 %collective-permute-done.1 = bf16[2,4,4,32,640]{4,3,2,1,0:T(8,128)(2,1)} collective-permute-done((bf16[2,4,4,32,640]{4,3,2,1,0:T(8,128)(2,1)}, bf16[2,4,4,32,640]{4,3,2,1,0:T(8,128)(2,1)}, u32[]{:S(2)}, u32[]{:S(2)}) %collective-permute-start.1) | collective-permute-done | bytes 1310752 | tf_op jit(solution)/shard_map/while/body/eval_jaxpr/ppermute | solution.py:16
  1047.1 17.1 %conditional.5 = ((f32[4,10,128]{2,1,0:T(8,128)S(1)}, f32[4,10,128]{2,1,0:T(8,128)S(1)}, f32[4,10,128,64]{2,3,1,0:T(8,128)S(1)})) conditional(s32[]{:T(128)} %convert_element_type.114, (f32[4,10,128]{2,1,0:T(8,128)S(1)}, f32[4,10,128]{2,1,0:T(8,128)S(1)}, f32[4,10,128,64]{2,3,1,0:T(8,128)S(1)}) %get-tuple-element.368, ...), branch_computations={%region_17.17_spmd, %region_18.20_spmd} | conditional | flops 174018560 | bytes 28467260 | solution.py:138
  1073.1 24.9 %collective-permute-done = bf16[2,4,4,32,640]{4,3,2,1,0:T(8,128)(2,1)} collective-permute-done((bf16[2,4,4,32,640]{4,3,2,1,0:T(8,128)(2,1)}, bf16[2,4,4,32,640]{4,3,2,1,0:T(8,128)(2,1)}, u32[]{:S(2)}, u32[]{:S(2)}) %collective-permute-start) | collective-permute-done | bytes 1310752 | tf_op jit(solution)/shard_map/while/body/eval_jaxpr/ppermute | solution.py:16
  1098.0 28.7 %collective-permute-done.1 = bf16[2,4,4,32,640]{4,3,2,1,0:T(8,128)(2,1)} collective-permute-done((bf16[2,4,4,32,640]{4,3,2,1,0:T(8,128)(2,1)}, bf16[2,4,4,32,640]{4,3,2,1,0:T(8,128)(2,1)}, u32[]{:S(2)}, u32[]{:S(2)}) %collective-permute-start.1) | collective-permute-done | bytes 1310752 | tf_op jit(solution)/shard_map/while/body/eval_jaxpr/ppermute | solution.py:16
  1126.7 17.1 %conditional.5 = ((f32[4,10,128]{2,1,0:T(8,128)S(1)}, f32[4,10,128]{2,1,0:T(8,128)S(1)}, f32[4,10,128,64]{2,3,1,0:T(8,128)S(1)})) conditional(s32[]{:T(128)} %convert_element_type.114, (f32[4,10,128]{2,1,0:T(8,128)S(1)}, f32[4,10,128]{2,1,0:T(8,128)S(1)}, f32[4,10,128,64]{2,3,1,0:T(8,128)S(1)}) %get-tuple-element.368, ...), branch_computations={%region_17.17_spmd, %region_18.20_spmd} | conditional | flops 174018560 | bytes 28467260 | solution.py:138
  1152.7 13.0 %collective-permute-done = bf16[2,4,4,32,640]{4,3,2,1,0:T(8,128)(2,1)} collective-permute-done((bf16[2,4,4,32,640]{4,3,2,1,0:T(8,128)(2,1)}, bf16[2,4,4,32,640]{4,3,2,1,0:T(8,128)(2,1)}, u32[]{:S(2)}, u32[]{:S(2)}) %collective-permute-start) | collective-permute-done | bytes 1310752 | tf_op jit(solution)/shard_map/while/body/eval_jaxpr/ppermute | solution.py:16
  1165.7 14.5 %collective-permute-done.1 = bf16[2,4,4,32,640]{4,3,2,1,0:T(8,128)(2,1)} collective-permute-done((bf16[2,4,4,32,640]{4,3,2,1,0:T(8,128)(2,1)}, bf16[2,4,4,32,640]{4,3,2,1,0:T(8,128)(2,1)}, u32[]{:S(2)}, u32[]{:S(2)}) %collective-permute-start.1) | collective-permute-done | bytes 1310752 | tf_op jit(solution)/shard_map/while/body/eval_jaxpr/ppermute | solution.py:16
  1180.2 17.1 %conditional.5 = ((f32[4,10,128]{2,1,0:T(8,128)S(1)}, f32[4,10,128]{2,1,0:T(8,128)S(1)}, f32[4,10,128,64]{2,3,1,0:T(8,128)S(1)})) conditional(s32[]{:T(128)} %convert_element_type.114, (f32[4,10,128]{2,1,0:T(8,128)S(1)}, f32[4,10,128]{2,1,0:T(8,128)S(1)}, f32[4,10,128,64]{2,3,1,0:T(8,128)S(1)}) %get-tuple-element.368, ...), branch_computations={%region_17.17_spmd, %region_18.20_spmd} | conditional | flops 174018560 | bytes 28467260 | solution.py:138
  1206.2 13.0 %collective-permute-done = bf16[2,4,4,32,640]{4,3,2,1,0:T(8,128)(2,1)} collective-permute-done((bf16[2,4,4,32,640]{4,3,2,1,0:T(8,128)(2,1)}, bf16[2,4,4,32,640]{4,3,2,1,0:T(8,128)(2,1)}, u32[]{:S(2)}, u32[]{:S(2)}) %collective-permute-start) | collective-permute-done | bytes 1310752 | tf_op jit(solution)/shard_map/while/body/eval_jaxpr/ppermute | solution.py:16
  1219.2 14.5 %collective-permute-done.1 = bf16[2,4,4,32,640]{4,3,2,1,0:T(8,128)(2,1)} collective-permute-done((bf16[2,4,4,32,640]{4,3,2,1,0:T(8,128)(2,1)}, bf16[2,4,4,32,640]{4,3,2,1,0:T(8,128)(2,1)}, u32[]{:S(2)}, u32[]{:S(2)}) %collective-permute-start.1) | collective-permute-done | bytes 1310752 | tf_op jit(solution)/shard_map/while/body/eval_jaxpr/ppermute | solution.py:16
  1233.7 17.1 %conditional.5 = ((f32[4,10,128]{2,1,0:T(8,128)S(1)}, f32[4,10,128]{2,1,0:T(8,128)S(1)}, f32[4,10,128,64]{2,3,1,0:T(8,128)S(1)})) conditional(s32[]{:T(128)} %convert_element_type.114, (f32[4,10,128]{2,1,0:T(8,128)S(1)}, f32[4,10,128]{2,1,0:T(8,128)S(1)}, f32[4,10,128,64]{2,3,1,0:T(8,128)S(1)}) %get-tuple-element.368, ...), branch_computations={%region_17.17_spmd, %region_18.20_spmd} | conditional | flops 174018560 | bytes 28467260 | solution.py:138
  (197 shorter events, 256.6 us)
Async XLA Ops:
  0.6 1264.7 %copy-start = (bf16[640,1280]{1,0:T(8,128)(2,1)S(1)}, bf16[640,1280]{1,0:T(8,128)(2,1)}, u32[]{:S(2)}) copy-start(bf16[640,1280]{1,0:T(8,128)(2,1)} %param.25) | copy-start | bytes 4915204
  0.6 10.7 copy-start.4
  4.1 711.9 %collective-permute-start.2 = (bf16[4,1,32,1280]{3,2,1,0:T(8,128)(2,1)}, bf16[4,1,32,1280]{3,2,1,0:T(8,128)(2,1)}, u32[]{:S(2)}, u32[]{:S(2)}) collective-permute-start(bf16[4,1,32,1280]{3,2,1,0:T(8,128)(2,1)} %get-tuple-element.259), channel_id=1, source_target_pairs={{0,8},{1,9},{2,10},{3,11},{4,12},{5,13},{6,14},{7,15},{8,16},{9,17... | collective-permute-start | bytes 983048 | tf_op jit(solution)/shard_map/ppermute | solution.py:16
  10.0 706.0 %collective-permute-start.3 = (bf16[4,1,32,1280]{3,2,1,0:T(8,128)(2,1)S(1)}, bf16[4,1,32,1280]{3,2,1,0:T(8,128)(2,1)}, u32[]{:S(2)}, u32[]{:S(2)}) collective-permute-start(bf16[4,1,32,1280]{3,2,1,0:T(8,128)(2,1)S(1)} %get-tuple-element.260), channel_id=1, source_target_pairs={{8,0},{9,1},{10,2},{11,3},{12,4},{13,5},{14,6},{15,7},{16,8},{17,9... | collective-permute-start | bytes 983048 | tf_op jit(solution)/shard_map/ppermute | solution.py:16
  365.8 345.2 %copy-start.19 = (s32[4,8]{1,0:T(4,128)S(1)}, s32[4,8]{1,0:T(4,128)}, u32[]{:S(2)}) copy-start(s32[4,8]{1,0:T(4,128)} %param.19) | copy-start | bytes 388
  365.8 345.5 %copy-start.17 = (f32[1280]{0:T(1024)S(1)}, f32[1280]{0:T(1024)}, u32[]{:S(2)}) copy-start(f32[1280]{0:T(1024)} %param.21) | copy-start | bytes 15364
  365.9 345.5 %copy-start.18 = (f32[1280]{0:T(1024)S(1)}, f32[1280]{0:T(1024)}, u32[]{:S(2)}) copy-start(f32[1280]{0:T(1024)} %param.20) | copy-start | bytes 15364
  713.2 8.4 copy-start.14
  730.6 6.4 copy-start.5
  743.0 5.9 copy-start.3
  753.3 29.9 %collective-permute-start = (bf16[2,4,4,32,640]{4,3,2,1,0:T(8,128)(2,1)}, bf16[2,4,4,32,640]{4,3,2,1,0:T(8,128)(2,1)}, u32[]{:S(2)}, u32[]{:S(2)}) collective-permute-start(bf16[2,4,4,32,640]{4,3,2,1,0:T(8,128)(2,1)} %get-tuple-element.349), channel_id=1, source_target_pairs={{0,8},{1,9},{2,10},{3,11},{4,12},{5,13},{6,14},{7,15},{8,16},{9,17... | collective-permute-start | bytes 3932168 | tf_op jit(solution)/shard_map/while/body/eval_jaxpr/ppermute | solution.py:16
  755.7 33.3 %collective-permute-start.1 = (bf16[2,4,4,32,640]{4,3,2,1,0:T(8,128)(2,1)}, bf16[2,4,4,32,640]{4,3,2,1,0:T(8,128)(2,1)}, u32[]{:S(2)}, u32[]{:S(2)}) collective-permute-start(bf16[2,4,4,32,640]{4,3,2,1,0:T(8,128)(2,1)} %get-tuple-element.350), channel_id=1, source_target_pairs={{8,0},{9,1},{10,2},{11,3},{12,4},{13,5},{14,6},{15,7},{16,8},{17,9... | collective-permute-start | bytes 3932168 | tf_op jit(solution)/shard_map/while/body/eval_jaxpr/ppermute | solution.py:16
  811.1 46.2 %collective-permute-start = (bf16[2,4,4,32,640]{4,3,2,1,0:T(8,128)(2,1)}, bf16[2,4,4,32,640]{4,3,2,1,0:T(8,128)(2,1)}, u32[]{:S(2)}, u32[]{:S(2)}) collective-permute-start(bf16[2,4,4,32,640]{4,3,2,1,0:T(8,128)(2,1)} %get-tuple-element.349), channel_id=1, source_target_pairs={{0,8},{1,9},{2,10},{3,11},{4,12},{5,13},{6,14},{7,15},{8,16},{9,17... | collective-permute-start | bytes 3932168 | tf_op jit(solution)/shard_map/while/body/eval_jaxpr/ppermute | solution.py:16
  829.5 56.7 %collective-permute-start.1 = (bf16[2,4,4,32,640]{4,3,2,1,0:T(8,128)(2,1)}, bf16[2,4,4,32,640]{4,3,2,1,0:T(8,128)(2,1)}, u32[]{:S(2)}, u32[]{:S(2)}) collective-permute-start(bf16[2,4,4,32,640]{4,3,2,1,0:T(8,128)(2,1)} %get-tuple-element.350), channel_id=1, source_target_pairs={{8,0},{9,1},{10,2},{11,3},{12,4},{13,5},{14,6},{15,7},{16,8},{17,9... | collective-permute-start | bytes 3932168 | tf_op jit(solution)/shard_map/while/body/eval_jaxpr/ppermute | solution.py:16
  908.3 29.9 %collective-permute-start = (bf16[2,4,4,32,640]{4,3,2,1,0:T(8,128)(2,1)}, bf16[2,4,4,32,640]{4,3,2,1,0:T(8,128)(2,1)}, u32[]{:S(2)}, u32[]{:S(2)}) collective-permute-start(bf16[2,4,4,32,640]{4,3,2,1,0:T(8,128)(2,1)} %get-tuple-element.349), channel_id=1, source_target_pairs={{0,8},{1,9},{2,10},{3,11},{4,12},{5,13},{6,14},{7,15},{8,16},{9,17... | collective-permute-start | bytes 3932168 | tf_op jit(solution)/shard_map/while/body/eval_jaxpr/ppermute | solution.py:16
  910.8 56.1 %collective-permute-start.1 = (bf16[2,4,4,32,640]{4,3,2,1,0:T(8,128)(2,1)}, bf16[2,4,4,32,640]{4,3,2,1,0:T(8,128)(2,1)}, u32[]{:S(2)}, u32[]{:S(2)}) collective-permute-start(bf16[2,4,4,32,640]{4,3,2,1,0:T(8,128)(2,1)} %get-tuple-element.350), channel_id=1, source_target_pairs={{8,0},{9,1},{10,2},{11,3},{12,4},{13,5},{14,6},{15,7},{16,8},{17,9... | collective-permute-start | bytes 3932168 | tf_op jit(solution)/shard_map/while/body/eval_jaxpr/ppermute | solution.py:16
  989.0 29.4 %collective-permute-start = (bf16[2,4,4,32,640]{4,3,2,1,0:T(8,128)(2,1)}, bf16[2,4,4,32,640]{4,3,2,1,0:T(8,128)(2,1)}, u32[]{:S(2)}, u32[]{:S(2)}) collective-permute-start(bf16[2,4,4,32,640]{4,3,2,1,0:T(8,128)(2,1)} %get-tuple-element.349), channel_id=1, source_target_pairs={{0,8},{1,9},{2,10},{3,11},{4,12},{5,13},{6,14},{7,15},{8,16},{9,17... | collective-permute-start | bytes 3932168 | tf_op jit(solution)/shard_map/while/body/eval_jaxpr/ppermute | solution.py:16
  991.6 55.5 %collective-permute-start.1 = (bf16[2,4,4,32,640]{4,3,2,1,0:T(8,128)(2,1)}, bf16[2,4,4,32,640]{4,3,2,1,0:T(8,128)(2,1)}, u32[]{:S(2)}, u32[]{:S(2)}) collective-permute-start(bf16[2,4,4,32,640]{4,3,2,1,0:T(8,128)(2,1)} %get-tuple-element.350), channel_id=1, source_target_pairs={{8,0},{9,1},{10,2},{11,3},{12,4},{13,5},{14,6},{15,7},{16,8},{17,9... | collective-permute-start | bytes 3932168 | tf_op jit(solution)/shard_map/while/body/eval_jaxpr/ppermute | solution.py:16
  1069.3 28.7 %collective-permute-start = (bf16[2,4,4,32,640]{4,3,2,1,0:T(8,128)(2,1)}, bf16[2,4,4,32,640]{4,3,2,1,0:T(8,128)(2,1)}, u32[]{:S(2)}, u32[]{:S(2)}) collective-permute-start(bf16[2,4,4,32,640]{4,3,2,1,0:T(8,128)(2,1)} %get-tuple-element.349), channel_id=1, source_target_pairs={{0,8},{1,9},{2,10},{3,11},{4,12},{5,13},{6,14},{7,15},{8,16},{9,17... | collective-permute-start | bytes 3932168 | tf_op jit(solution)/shard_map/while/body/eval_jaxpr/ppermute | solution.py:16
  1071.8 54.9 %collective-permute-start.1 = (bf16[2,4,4,32,640]{4,3,2,1,0:T(8,128)(2,1)}, bf16[2,4,4,32,640]{4,3,2,1,0:T(8,128)(2,1)}, u32[]{:S(2)}, u32[]{:S(2)}) collective-permute-start(bf16[2,4,4,32,640]{4,3,2,1,0:T(8,128)(2,1)} %get-tuple-element.350), channel_id=1, source_target_pairs={{8,0},{9,1},{10,2},{11,3},{12,4},{13,5},{14,6},{15,7},{16,8},{17,9... | collective-permute-start | bytes 3932168 | tf_op jit(solution)/shard_map/while/body/eval_jaxpr/ppermute | solution.py:16
  1148.9 16.9 %collective-permute-start = (bf16[2,4,4,32,640]{4,3,2,1,0:T(8,128)(2,1)}, bf16[2,4,4,32,640]{4,3,2,1,0:T(8,128)(2,1)}, u32[]{:S(2)}, u32[]{:S(2)}) collective-permute-start(bf16[2,4,4,32,640]{4,3,2,1,0:T(8,128)(2,1)} %get-tuple-element.349), channel_id=1, source_target_pairs={{0,8},{1,9},{2,10},{3,11},{4,12},{5,13},{6,14},{7,15},{8,16},{9,17... | collective-permute-start | bytes 3932168 | tf_op jit(solution)/shard_map/while/body/eval_jaxpr/ppermute | solution.py:16
  1151.4 28.8 %collective-permute-start.1 = (bf16[2,4,4,32,640]{4,3,2,1,0:T(8,128)(2,1)}, bf16[2,4,4,32,640]{4,3,2,1,0:T(8,128)(2,1)}, u32[]{:S(2)}, u32[]{:S(2)}) collective-permute-start(bf16[2,4,4,32,640]{4,3,2,1,0:T(8,128)(2,1)} %get-tuple-element.350), channel_id=1, source_target_pairs={{8,0},{9,1},{10,2},{11,3},{12,4},{13,5},{14,6},{15,7},{16,8},{17,9... | collective-permute-start | bytes 3932168 | tf_op jit(solution)/shard_map/while/body/eval_jaxpr/ppermute | solution.py:16
  1202.4 16.9 %collective-permute-start = (bf16[2,4,4,32,640]{4,3,2,1,0:T(8,128)(2,1)}, bf16[2,4,4,32,640]{4,3,2,1,0:T(8,128)(2,1)}, u32[]{:S(2)}, u32[]{:S(2)}) collective-permute-start(bf16[2,4,4,32,640]{4,3,2,1,0:T(8,128)(2,1)} %get-tuple-element.349), channel_id=1, source_target_pairs={{0,8},{1,9},{2,10},{3,11},{4,12},{5,13},{6,14},{7,15},{8,16},{9,17... | collective-permute-start | bytes 3932168 | tf_op jit(solution)/shard_map/while/body/eval_jaxpr/ppermute | solution.py:16
  1204.9 28.8 %collective-permute-start.1 = (bf16[2,4,4,32,640]{4,3,2,1,0:T(8,128)(2,1)}, bf16[2,4,4,32,640]{4,3,2,1,0:T(8,128)(2,1)}, u32[]{:S(2)}, u32[]{:S(2)}) collective-permute-start(bf16[2,4,4,32,640]{4,3,2,1,0:T(8,128)(2,1)} %get-tuple-element.350), channel_id=1, source_target_pairs={{8,0},{9,1},{10,2},{11,3},{12,4},{13,5},{14,6},{15,7},{16,8},{17,9... | collective-permute-start | bytes 3932168 | tf_op jit(solution)/shard_map/while/body/eval_jaxpr/ppermute | solution.py:16
  (17 other events, 31.9 us)
where the time goes:
time: 1270 us
  blocking collectives  693 us (55%)
  waiting for transfers between devices  305 us (24%)
  local copies, waits for them, and re-layouts  141 us (11%)
  matrix products  63.4 us (5%)
  starting transfers between devices  49.7 us (4%)
  other arithmetic  14.6 us (1%)
    psum x1, blocking collectives, on_device(): totals = lax.psum(slot_mask * jnp.sum(grouped, axis=(1, 3))[None], 'band')  351 us
    psum x1, blocking collectives, on_device(): lax.psum(slot_mask * jnp.sum(deviation * deviation, axis=(1, 3))[None], '...  342 us
    ppermute x16, waiting for transfers between devices, shifted(): return lax.ppermute(value, axis, pairs)  305 us
    ppermute x16, starting transfers between devices, shifted(): return lax.ppermute(value, axis, pairs)  49.7 us
    while x14, local copies, waits for them, and re-layouts  35.1 us
  transfers between devices with their start and end apart: 16, of which 14 were waited for; matrix products, arithmetic and copies ran while one was open for 1% of the time, Pallas kernels for 0%

commit v1 on v0

--- a/solution.py
+++ b/solution.py
@@ -70,7 +70,10 @@
     totals = lax.psum(slot_mask * jnp.sum(grouped, axis=(1, 3))[None], "band")
     center = jnp.sum(totals * slot_mask, axis=0) / counted
     deviation = grouped - center[:, None, :, None]
-    spreads = lax.psum(slot_mask * jnp.sum(deviation * deviation, axis=(1, 3))[None], "band")
+    spreads = jnp.sum(
+        lax.all_gather(slot_mask * jnp.sum(deviation * deviation, axis=(1, 3))[None], "band"),
+        axis=0,
+    )
     spread = jnp.sum(spreads * slot_mask, axis=0) / counted
     normed = (
         (grouped - center[:, None, :, None]) / jnp.sqrt(spread + 1e-05)[:, None, :, None]

time: 1270 us -> 1090 us (0.86)
  blocking collectives: 693 us -> 536 us
  waiting for transfers between devices: 305 us -> 263 us
    psum x1 -> x0, blocking collectives: 342 us -> none  [on_device(): lax.psum(slot_mask * jnp.sum(deviation * deviation, axis=(1, 3))[None], '...]
    all_gather x0 -> x1, blocking collectives: none -> 185 us  [on_device(): lax.all_gather(slot_mask * jnp.sum(deviation * deviation, axis=(1, 3))[No...]
    ppermute x16, waiting for transfers between devices: 305 us -> 263 us  [shifted(): return lax.ppermute(value, axis, pairs)]
where the time goes in v1:
time: 1090 us; the launch traced here: 1080 us
  blocking collectives  536 us (49%)
  waiting for transfers between devices  263 us (24%)
  local copies, waits for them, and re-layouts  141 us (13%)
  matrix products  63.4 us (6%)
  starting transfers between devices  54.6 us (5%)
  other arithmetic  16 us (1%)
    psum x1, blocking collectives, on_device(): totals = lax.psum(slot_mask * jnp.sum(grouped, axis=(1, 3))[None], 'band')  351 us
    ppermute x16, waiting for transfers between devices, shifted(): return lax.ppermute(value, axis, pairs)  263 us
    all_gather x1, blocking collectives, on_device(): lax.all_gather(slot_mask * jnp.sum(deviation * deviation, axis=(1, 3))[No...  185 us
    ppermute x16, starting transfers between devices, shifted(): return lax.ppermute(value, axis, pairs)  54.6 us
    while x14, local copies, waits for them, and re-layouts  35.1 us
    squeeze x7, local copies, waits for them, and re-layouts, absorb(): piece[0].reshape(images, piece_rows * columns, head_count, head_size)  24.8 us
    squeeze x7, local copies, waits for them, and re-layouts, absorb(): piece[1].reshape(images, piece_rows * columns, head_count, head_size)  24.8 us
    dot_general x8, matrix products, attend_block(): jnp.einsum('bhqk,bkhd->bhqd', exponent.astype(jnp.bfloat16), values, pref...  23.1 us
  transfers between devices with their start and end apart: 16, of which 14 were waited for; matrix products, arithmetic and copies ran while one was open for 1% of the time, Pallas kernels for 0%

profile of v1, /device:TPU:0, one launch (start us, length us, event | category | flops | bytes accessed | tf_op | source)
XLA Modules:
  0.0 1075.8 jit_solution(10062161369199987397)
XLA Ops:
  14.5 351.0 %psum.7 = f32[8,4,32]{2,0,1:T(8,128)S(1)} all-reduce(f32[8,4,32]{2,0,1:T(8,128)S(1)} %broadcast_multiply_fusion.1), channel_id=1, replica_groups=mesh['img'=2,'band'=64] {'band'}, use_global_device_ids=true, to_apply=%region_2.3 | all-reduce | flops 1024 | bytes 8192 | tf_op jit(solution)/shard_map/psum | solution.py:70
  366.5 185.2 %all_gather.4 = f32[64,8,4,32]{3,1,2,0:T(8,128)} all-gather(f32[1,8,4,32]{3,1,2,0:T(8,128)S(1)} %broadcast_multiply_fusion), channel_id=1, replica_groups=mesh['img'=2,'band'=64] {'band'}, dimensions={0}, use_global_device_ids=true | all-gather | bytes 266240 | tf_op jit(solution)/shard_map/all_gather | solution.py:74
  598.2 465.2 %while.21 = (s32[]{:T(128)}, bf16[2,4,4,32,640]{4,3,2,1,0:T(8,128)(2,1)}, bf16[2,4,4,32,640]{4,3,2,1,0:T(8,128)(2,1)}, f32[4,10,128]{2,1,0:T(8,128)S(1)}, f32[4,...) while((s32[]{:T(128)}, ...), condition=%wide.region_21.22_spmd, body=%wide.region_12.21_spmd.sunk | while | flops 348037120 | bytes 72663480 | solution.py:146
  601.9 13.0 %collective-permute-done = bf16[2,4,4,32,640]{4,3,2,1,0:T(8,128)(2,1)} collective-permute-done((bf16[2,4,4,32,640]{4,3,2,1,0:T(8,128)(2,1)}, bf16[2,4,4,32,640]{4,3,2,1,0:T(8,128)(2,1)}, u32[]{:S(2)}, u32[]{:S(2)}) %collective-permute-start) | collective-permute-done | bytes 1310752 | tf_op jit(solution)/shard_map/while/body/eval_jaxpr/ppermute | solution.py:16
  614.9 19.3 %collective-permute-done.1 = bf16[2,4,4,32,640]{4,3,2,1,0:T(8,128)(2,1)} collective-permute-done((bf16[2,4,4,32,640]{4,3,2,1,0:T(8,128)(2,1)}, bf16[2,4,4,32,640]{4,3,2,1,0:T(8,128)(2,1)}, u32[]{:S(2)}, u32[]{:S(2)}) %collective-permute-start.1) | collective-permute-done | bytes 1310752 | tf_op jit(solution)/shard_map/while/body/eval_jaxpr/ppermute | solution.py:16
  634.2 17.1 %conditional.5 = ((f32[4,10,128]{2,1,0:T(8,128)S(1)}, f32[4,10,128]{2,1,0:T(8,128)S(1)}, f32[4,10,128,64]{2,3,1,0:T(8,128)S(1)})) conditional(s32[]{:T(128)} %convert_element_type.114, (f32[4,10,128]{2,1,0:T(8,128)S(1)}, f32[4,10,128]{2,1,0:T(8,128)S(1)}, f32[4,10,128,64]{2,3,1,0:T(8,128)S(1)}) %get-tuple-element.384, ...), branch_computations={%region_17.17_spmd, %region_18.20_spmd} | conditional | flops 174018560 | bytes 28467260 | solution.py:141
  662.4 16.6 %collective-permute-done = bf16[2,4,4,32,640]{4,3,2,1,0:T(8,128)(2,1)} collective-permute-done((bf16[2,4,4,32,640]{4,3,2,1,0:T(8,128)(2,1)}, bf16[2,4,4,32,640]{4,3,2,1,0:T(8,128)(2,1)}, u32[]{:S(2)}, u32[]{:S(2)}) %collective-permute-start) | collective-permute-done | bytes 1310752 | tf_op jit(solution)/shard_map/while/body/eval_jaxpr/ppermute | solution.py:16
  679.0 28.7 %collective-permute-done.1 = bf16[2,4,4,32,640]{4,3,2,1,0:T(8,128)(2,1)} collective-permute-done((bf16[2,4,4,32,640]{4,3,2,1,0:T(8,128)(2,1)}, bf16[2,4,4,32,640]{4,3,2,1,0:T(8,128)(2,1)}, u32[]{:S(2)}, u32[]{:S(2)}) %collective-permute-start.1) | collective-permute-done | bytes 1310752 | tf_op jit(solution)/shard_map/while/body/eval_jaxpr/ppermute | solution.py:16
  707.7 17.1 %conditional.5 = ((f32[4,10,128]{2,1,0:T(8,128)S(1)}, f32[4,10,128]{2,1,0:T(8,128)S(1)}, f32[4,10,128,64]{2,3,1,0:T(8,128)S(1)})) conditional(s32[]{:T(128)} %convert_element_type.114, (f32[4,10,128]{2,1,0:T(8,128)S(1)}, f32[4,10,128]{2,1,0:T(8,128)S(1)}, f32[4,10,128,64]{2,3,1,0:T(8,128)S(1)}) %get-tuple-element.384, ...), branch_computations={%region_17.17_spmd, %region_18.20_spmd} | conditional | flops 174018560 | bytes 28467260 | solution.py:141
  733.7 15.9 %collective-permute-done = bf16[2,4,4,32,640]{4,3,2,1,0:T(8,128)(2,1)} collective-permute-done((bf16[2,4,4,32,640]{4,3,2,1,0:T(8,128)(2,1)}, bf16[2,4,4,32,640]{4,3,2,1,0:T(8,128)(2,1)}, u32[]{:S(2)}, u32[]{:S(2)}) %collective-permute-start) | collective-permute-done | bytes 1310752 | tf_op jit(solution)/shard_map/while/body/eval_jaxpr/ppermute | solution.py:16
  749.7 28.7 %collective-permute-done.1 = bf16[2,4,4,32,640]{4,3,2,1,0:T(8,128)(2,1)} collective-permute-done((bf16[2,4,4,32,640]{4,3,2,1,0:T(8,128)(2,1)}, bf16[2,4,4,32,640]{4,3,2,1,0:T(8,128)(2,1)}, u32[]{:S(2)}, u32[]{:S(2)}) %collective-permute-start.1) | collective-permute-done | bytes 1310752 | tf_op jit(solution)/shard_map/while/body/eval_jaxpr/ppermute | solution.py:16
  778.4 17.1 %conditional.5 = ((f32[4,10,128]{2,1,0:T(8,128)S(1)}, f32[4,10,128]{2,1,0:T(8,128)S(1)}, f32[4,10,128,64]{2,3,1,0:T(8,128)S(1)})) conditional(s32[]{:T(128)} %convert_element_type.114, (f32[4,10,128]{2,1,0:T(8,128)S(1)}, f32[4,10,128]{2,1,0:T(8,128)S(1)}, f32[4,10,128,64]{2,3,1,0:T(8,128)S(1)}) %get-tuple-element.384, ...), branch_computations={%region_17.17_spmd, %region_18.20_spmd} | conditional | flops 174018560 | bytes 28467260 | solution.py:141
  804.3 13.0 %collective-permute-done = bf16[2,4,4,32,640]{4,3,2,1,0:T(8,128)(2,1)} collective-permute-done((bf16[2,4,4,32,640]{4,3,2,1,0:T(8,128)(2,1)}, bf16[2,4,4,32,640]{4,3,2,1,0:T(8,128)(2,1)}, u32[]{:S(2)}, u32[]{:S(2)}) %collective-permute-start) | collective-permute-done | bytes 1310752 | tf_op jit(solution)/shard_map/while/body/eval_jaxpr/ppermute | solution.py:16
  817.4 26.6 %collective-permute-done.1 = bf16[2,4,4,32,640]{4,3,2,1,0:T(8,128)(2,1)} collective-permute-done((bf16[2,4,4,32,640]{4,3,2,1,0:T(8,128)(2,1)}, bf16[2,4,4,32,640]{4,3,2,1,0:T(8,128)(2,1)}, u32[]{:S(2)}, u32[]{:S(2)}) %collective-permute-start.1) | collective-permute-done | bytes 1310752 | tf_op jit(solution)/shard_map/while/body/eval_jaxpr/ppermute | solution.py:16
  844.0 17.1 %conditional.5 = ((f32[4,10,128]{2,1,0:T(8,128)S(1)}, f32[4,10,128]{2,1,0:T(8,128)S(1)}, f32[4,10,128,64]{2,3,1,0:T(8,128)S(1)})) conditional(s32[]{:T(128)} %convert_element_type.114, (f32[4,10,128]{2,1,0:T(8,128)S(1)}, f32[4,10,128]{2,1,0:T(8,128)S(1)}, f32[4,10,128,64]{2,3,1,0:T(8,128)S(1)}) %get-tuple-element.384, ...), branch_computations={%region_17.17_spmd, %region_18.20_spmd} | conditional | flops 174018560 | bytes 28467260 | solution.py:141
  870.0 13.0 %collective-permute-done = bf16[2,4,4,32,640]{4,3,2,1,0:T(8,128)(2,1)} collective-permute-done((bf16[2,4,4,32,640]{4,3,2,1,0:T(8,128)(2,1)}, bf16[2,4,4,32,640]{4,3,2,1,0:T(8,128)(2,1)}, u32[]{:S(2)}, u32[]{:S(2)}) %collective-permute-start) | collective-permute-done | bytes 1310752 | tf_op jit(solution)/shard_map/while/body/eval_jaxpr/ppermute | solution.py:16
  883.0 32.7 %collective-permute-done.1 = bf16[2,4,4,32,640]{4,3,2,1,0:T(8,128)(2,1)} collective-permute-done((bf16[2,4,4,32,640]{4,3,2,1,0:T(8,128)(2,1)}, bf16[2,4,4,32,640]{4,3,2,1,0:T(8,128)(2,1)}, u32[]{:S(2)}, u32[]{:S(2)}) %collective-permute-start.1) | collective-permute-done | bytes 1310752 | tf_op jit(solution)/shard_map/while/body/eval_jaxpr/ppermute | solution.py:16
  915.7 17.1 %conditional.5 = ((f32[4,10,128]{2,1,0:T(8,128)S(1)}, f32[4,10,128]{2,1,0:T(8,128)S(1)}, f32[4,10,128,64]{2,3,1,0:T(8,128)S(1)})) conditional(s32[]{:T(128)} %convert_element_type.114, (f32[4,10,128]{2,1,0:T(8,128)S(1)}, f32[4,10,128]{2,1,0:T(8,128)S(1)}, f32[4,10,128,64]{2,3,1,0:T(8,128)S(1)}) %get-tuple-element.384, ...), branch_computations={%region_17.17_spmd, %region_18.20_spmd} | conditional | flops 174018560 | bytes 28467260 | solution.py:141
  937.8 21.1 %collective-permute-start = (bf16[2,4,4,32,640]{4,3,2,1,0:T(8,128)(2,1)}, bf16[2,4,4,32,640]{4,3,2,1,0:T(8,128)(2,1)}, u32[]{:S(2)}, u32[]{:S(2)}) collective-permute-start(bf16[2,4,4,32,640]{4,3,2,1,0:T(8,128)(2,1)} %get-tuple-element.365), channel_id=1, source_target_pairs={{0,8},{1,9},{2,10},{3,11},{4,12},{5,13},{6,14},{7,15},{8,16},{9,17... | collective-permute-start | bytes 3932168 | tf_op jit(solution)/shard_map/while/body/eval_jaxpr/ppermute | solution.py:16
  960.2 13.0 %collective-permute-done = bf16[2,4,4,32,640]{4,3,2,1,0:T(8,128)(2,1)} collective-permute-done((bf16[2,4,4,32,640]{4,3,2,1,0:T(8,128)(2,1)}, bf16[2,4,4,32,640]{4,3,2,1,0:T(8,128)(2,1)}, u32[]{:S(2)}, u32[]{:S(2)}) %collective-permute-start) | collective-permute-done | bytes 1310752 | tf_op jit(solution)/shard_map/while/body/eval_jaxpr/ppermute | solution.py:16
  973.2 14.5 %collective-permute-done.1 = bf16[2,4,4,32,640]{4,3,2,1,0:T(8,128)(2,1)} collective-permute-done((bf16[2,4,4,32,640]{4,3,2,1,0:T(8,128)(2,1)}, bf16[2,4,4,32,640]{4,3,2,1,0:T(8,128)(2,1)}, u32[]{:S(2)}, u32[]{:S(2)}) %collective-permute-start.1) | collective-permute-done | bytes 1310752 | tf_op jit(solution)/shard_map/while/body/eval_jaxpr/ppermute | solution.py:16
  987.7 17.1 %conditional.5 = ((f32[4,10,128]{2,1,0:T(8,128)S(1)}, f32[4,10,128]{2,1,0:T(8,128)S(1)}, f32[4,10,128,64]{2,3,1,0:T(8,128)S(1)})) conditional(s32[]{:T(128)} %convert_element_type.114, (f32[4,10,128]{2,1,0:T(8,128)S(1)}, f32[4,10,128]{2,1,0:T(8,128)S(1)}, f32[4,10,128,64]{2,3,1,0:T(8,128)S(1)}) %get-tuple-element.384, ...), branch_computations={%region_17.17_spmd, %region_18.20_spmd} | conditional | flops 174018560 | bytes 28467260 | solution.py:141
  1026.7 14.5 %collective-permute-done.1 = bf16[2,4,4,32,640]{4,3,2,1,0:T(8,128)(2,1)} collective-permute-done((bf16[2,4,4,32,640]{4,3,2,1,0:T(8,128)(2,1)}, bf16[2,4,4,32,640]{4,3,2,1,0:T(8,128)(2,1)}, u32[]{:S(2)}, u32[]{:S(2)}) %collective-permute-start.1) | collective-permute-done | bytes 1310752 | tf_op jit(solution)/shard_map/while/body/eval_jaxpr/ppermute | solution.py:16
  1041.2 17.1 %conditional.5 = ((f32[4,10,128]{2,1,0:T(8,128)S(1)}, f32[4,10,128]{2,1,0:T(8,128)S(1)}, f32[4,10,128,64]{2,3,1,0:T(8,128)S(1)})) conditional(s32[]{:T(128)} %convert_element_type.114, (f32[4,10,128]{2,1,0:T(8,128)S(1)}, f32[4,10,128]{2,1,0:T(8,128)S(1)}, f32[4,10,128,64]{2,3,1,0:T(8,128)S(1)}) %get-tuple-element.384, ...), branch_computations={%region_17.17_spmd, %region_18.20_spmd} | conditional | flops 174018560 | bytes 28467260 | solution.py:141
  (198 shorter events, 267.4 us)
Async XLA Ops:
  0.6 1072.2 %copy-start = (bf16[640,1280]{1,0:T(8,128)(2,1)S(1)}, bf16[640,1280]{1,0:T(8,128)(2,1)}, u32[]{:S(2)}) copy-start(bf16[640,1280]{1,0:T(8,128)(2,1)} %param.25) | copy-start | bytes 4915204
  0.6 10.7 copy-start.4
  4.1 556.8 %collective-permute-start.2 = (bf16[4,1,32,1280]{3,2,1,0:T(8,128)(2,1)}, bf16[4,1,32,1280]{3,2,1,0:T(8,128)(2,1)}, u32[]{:S(2)}, u32[]{:S(2)}) collective-permute-start(bf16[4,1,32,1280]{3,2,1,0:T(8,128)(2,1)} %get-tuple-element.275), channel_id=1, source_target_pairs={{0,8},{1,9},{2,10},{3,11},{4,12},{5,13},{6,14},{7,15},{8,16},{9,17... | collective-permute-start | bytes 983048 | tf_op jit(solution)/shard_map/ppermute | solution.py:16
  10.0 550.9 %collective-permute-start.3 = (bf16[4,1,32,1280]{3,2,1,0:T(8,128)(2,1)S(1)}, bf16[4,1,32,1280]{3,2,1,0:T(8,128)(2,1)}, u32[]{:S(2)}, u32[]{:S(2)}) collective-permute-start(bf16[4,1,32,1280]{3,2,1,0:T(8,128)(2,1)S(1)} %get-tuple-element.276), channel_id=1, source_target_pairs={{8,0},{9,1},{10,2},{11,3},{12,4},{13,5},{14,6},{15,7},{16,8},{17,9... | collective-permute-start | bytes 983048 | tf_op jit(solution)/shard_map/ppermute | solution.py:16
  551.7 4.2 copy-start.19
  551.7 4.5 copy-start.17
  551.7 4.5 copy-start.18
  558.1 8.4 copy-start.14
  575.5 6.4 copy-start.5
  587.9 5.9 copy-start.3
  598.2 16.7 %collective-permute-start = (bf16[2,4,4,32,640]{4,3,2,1,0:T(8,128)(2,1)}, bf16[2,4,4,32,640]{4,3,2,1,0:T(8,128)(2,1)}, u32[]{:S(2)}, u32[]{:S(2)}) collective-permute-start(bf16[2,4,4,32,640]{4,3,2,1,0:T(8,128)(2,1)} %get-tuple-element.365), channel_id=1, source_target_pairs={{0,8},{1,9},{2,10},{3,11},{4,12},{5,13},{6,14},{7,15},{8,16},{9,17... | collective-permute-start | bytes 3932168 | tf_op jit(solution)/shard_map/while/body/eval_jaxpr/ppermute | solution.py:16
  600.6 33.7 %collective-permute-start.1 = (bf16[2,4,4,32,640]{4,3,2,1,0:T(8,128)(2,1)}, bf16[2,4,4,32,640]{4,3,2,1,0:T(8,128)(2,1)}, u32[]{:S(2)}, u32[]{:S(2)}) collective-permute-start(bf16[2,4,4,32,640]{4,3,2,1,0:T(8,128)(2,1)} %get-tuple-element.366), channel_id=1, source_target_pairs={{8,0},{9,1},{10,2},{11,3},{12,4},{13,5},{14,6},{15,7},{16,8},{17,9... | collective-permute-start | bytes 3932168 | tf_op jit(solution)/shard_map/while/body/eval_jaxpr/ppermute | solution.py:16
  656.3 22.7 %collective-permute-start = (bf16[2,4,4,32,640]{4,3,2,1,0:T(8,128)(2,1)}, bf16[2,4,4,32,640]{4,3,2,1,0:T(8,128)(2,1)}, u32[]{:S(2)}, u32[]{:S(2)}) collective-permute-start(bf16[2,4,4,32,640]{4,3,2,1,0:T(8,128)(2,1)} %get-tuple-element.365), channel_id=1, source_target_pairs={{0,8},{1,9},{2,10},{3,11},{4,12},{5,13},{6,14},{7,15},{8,16},{9,17... | collective-permute-start | bytes 3932168 | tf_op jit(solution)/shard_map/while/body/eval_jaxpr/ppermute | solution.py:16
  661.1 46.6 %collective-permute-start.1 = (bf16[2,4,4,32,640]{4,3,2,1,0:T(8,128)(2,1)}, bf16[2,4,4,32,640]{4,3,2,1,0:T(8,128)(2,1)}, u32[]{:S(2)}, u32[]{:S(2)}) collective-permute-start(bf16[2,4,4,32,640]{4,3,2,1,0:T(8,128)(2,1)} %get-tuple-element.366), channel_id=1, source_target_pairs={{8,0},{9,1},{10,2},{11,3},{12,4},{13,5},{14,6},{15,7},{16,8},{17,9... | collective-permute-start | bytes 3932168 | tf_op jit(solution)/shard_map/while/body/eval_jaxpr/ppermute | solution.py:16
  729.9 19.8 %collective-permute-start = (bf16[2,4,4,32,640]{4,3,2,1,0:T(8,128)(2,1)}, bf16[2,4,4,32,640]{4,3,2,1,0:T(8,128)(2,1)}, u32[]{:S(2)}, u32[]{:S(2)}) collective-permute-start(bf16[2,4,4,32,640]{4,3,2,1,0:T(8,128)(2,1)} %get-tuple-element.365), channel_id=1, source_target_pairs={{0,8},{1,9},{2,10},{3,11},{4,12},{5,13},{6,14},{7,15},{8,16},{9,17... | collective-permute-start | bytes 3932168 | tf_op jit(solution)/shard_map/while/body/eval_jaxpr/ppermute | solution.py:16
  732.4 45.9 %collective-permute-start.1 = (bf16[2,4,4,32,640]{4,3,2,1,0:T(8,128)(2,1)}, bf16[2,4,4,32,640]{4,3,2,1,0:T(8,128)(2,1)}, u32[]{:S(2)}, u32[]{:S(2)}) collective-permute-start(bf16[2,4,4,32,640]{4,3,2,1,0:T(8,128)(2,1)} %get-tuple-element.366), channel_id=1, source_target_pairs={{8,0},{9,1},{10,2},{11,3},{12,4},{13,5},{14,6},{15,7},{16,8},{17,9... | collective-permute-start | bytes 3932168 | tf_op jit(solution)/shard_map/while/body/eval_jaxpr/ppermute | solution.py:16
  800.5 16.9 %collective-permute-start = (bf16[2,4,4,32,640]{4,3,2,1,0:T(8,128)(2,1)}, bf16[2,4,4,32,640]{4,3,2,1,0:T(8,128)(2,1)}, u32[]{:S(2)}, u32[]{:S(2)}) collective-permute-start(bf16[2,4,4,32,640]{4,3,2,1,0:T(8,128)(2,1)} %get-tuple-element.365), channel_id=1, source_target_pairs={{0,8},{1,9},{2,10},{3,11},{4,12},{5,13},{6,14},{7,15},{8,16},{9,17... | collective-permute-start | bytes 3932168 | tf_op jit(solution)/shard_map/while/body/eval_jaxpr/ppermute | solution.py:16
  803.0 41.0 %collective-permute-start.1 = (bf16[2,4,4,32,640]{4,3,2,1,0:T(8,128)(2,1)}, bf16[2,4,4,32,640]{4,3,2,1,0:T(8,128)(2,1)}, u32[]{:S(2)}, u32[]{:S(2)}) collective-permute-start(bf16[2,4,4,32,640]{4,3,2,1,0:T(8,128)(2,1)} %get-tuple-element.366), channel_id=1, source_target_pairs={{8,0},{9,1},{10,2},{11,3},{12,4},{13,5},{14,6},{15,7},{16,8},{17,9... | collective-permute-start | bytes 3932168 | tf_op jit(solution)/shard_map/while/body/eval_jaxpr/ppermute | solution.py:16
  866.1 16.9 %collective-permute-start = (bf16[2,4,4,32,640]{4,3,2,1,0:T(8,128)(2,1)}, bf16[2,4,4,32,640]{4,3,2,1,0:T(8,128)(2,1)}, u32[]{:S(2)}, u32[]{:S(2)}) collective-permute-start(bf16[2,4,4,32,640]{4,3,2,1,0:T(8,128)(2,1)} %get-tuple-element.365), channel_id=1, source_target_pairs={{0,8},{1,9},{2,10},{3,11},{4,12},{5,13},{6,14},{7,15},{8,16},{9,17... | collective-permute-start | bytes 3932168 | tf_op jit(solution)/shard_map/while/body/eval_jaxpr/ppermute | solution.py:16
  868.7 47.0 %collective-permute-start.1 = (bf16[2,4,4,32,640]{4,3,2,1,0:T(8,128)(2,1)}, bf16[2,4,4,32,640]{4,3,2,1,0:T(8,128)(2,1)}, u32[]{:S(2)}, u32[]{:S(2)}) collective-permute-start(bf16[2,4,4,32,640]{4,3,2,1,0:T(8,128)(2,1)} %get-tuple-element.366), channel_id=1, source_target_pairs={{8,0},{9,1},{10,2},{11,3},{12,4},{13,5},{14,6},{15,7},{16,8},{17,9... | collective-permute-start | bytes 3932168 | tf_op jit(solution)/shard_map/while/body/eval_jaxpr/ppermute | solution.py:16
  937.8 35.4 %collective-permute-start = (bf16[2,4,4,32,640]{4,3,2,1,0:T(8,128)(2,1)}, bf16[2,4,4,32,640]{4,3,2,1,0:T(8,128)(2,1)}, u32[]{:S(2)}, u32[]{:S(2)}) collective-permute-start(bf16[2,4,4,32,640]{4,3,2,1,0:T(8,128)(2,1)} %get-tuple-element.365), channel_id=1, source_target_pairs={{0,8},{1,9},{2,10},{3,11},{4,12},{5,13},{6,14},{7,15},{8,16},{9,17... | collective-permute-start | bytes 3932168 | tf_op jit(solution)/shard_map/while/body/eval_jaxpr/ppermute | solution.py:16
  958.9 28.8 %collective-permute-start.1 = (bf16[2,4,4,32,640]{4,3,2,1,0:T(8,128)(2,1)}, bf16[2,4,4,32,640]{4,3,2,1,0:T(8,128)(2,1)}, u32[]{:S(2)}, u32[]{:S(2)}) collective-permute-start(bf16[2,4,4,32,640]{4,3,2,1,0:T(8,128)(2,1)} %get-tuple-element.366), channel_id=1, source_target_pairs={{8,0},{9,1},{10,2},{11,3},{12,4},{13,5},{14,6},{15,7},{16,8},{17,9... | collective-permute-start | bytes 3932168 | tf_op jit(solution)/shard_map/while/body/eval_jaxpr/ppermute | solution.py:16
  1009.8 16.9 %collective-permute-start = (bf16[2,4,4,32,640]{4,3,2,1,0:T(8,128)(2,1)}, bf16[2,4,4,32,640]{4,3,2,1,0:T(8,128)(2,1)}, u32[]{:S(2)}, u32[]{:S(2)}) collective-permute-start(bf16[2,4,4,32,640]{4,3,2,1,0:T(8,128)(2,1)} %get-tuple-element.365), channel_id=1, source_target_pairs={{0,8},{1,9},{2,10},{3,11},{4,12},{5,13},{6,14},{7,15},{8,16},{9,17... | collective-permute-start | bytes 3932168 | tf_op jit(solution)/shard_map/while/body/eval_jaxpr/ppermute | solution.py:16
  1012.4 28.8 %collective-permute-start.1 = (bf16[2,4,4,32,640]{4,3,2,1,0:T(8,128)(2,1)}, bf16[2,4,4,32,640]{4,3,2,1,0:T(8,128)(2,1)}, u32[]{:S(2)}, u32[]{:S(2)}) collective-permute-start(bf16[2,4,4,32,640]{4,3,2,1,0:T(8,128)(2,1)} %get-tuple-element.366), channel_id=1, source_target_pairs={{8,0},{9,1},{10,2},{11,3},{12,4},{13,5},{14,6},{15,7},{16,8},{17,9... | collective-permute-start | bytes 3932168 | tf_op jit(solution)/shard_map/while/body/eval_jaxpr/ppermute | solution.py:16
  (17 other events, 31.9 us)
